TPU v7x, 32 devices: a whole 2x2x4 slice. The times are simulated.
32 devices in a mesh: grp: 2 (over y), seq: 16 (over z, x, core).
Axes of the slice: x: 2, y: 2, z: 4, core: 2. Of those that a mesh axis runs over, the one named last changes fastest.
Arguments:
- inputs: bfloat16 [4, 2048, 1536], P('grp', 'seq'), parts along dimension 0, may hold values from -36 to 36
- gain: float32 [1536], replicated, may hold values from 0.1 to 1.9
- conv_weight: bfloat16 [3, 1536, 768], P(None, 'seq'), may hold values from -0.09375 to 0.09375
- proj_weight: bfloat16 [768, 1536], P(None, 'seq'), may hold values from -0.21875 to 0.21875
- head_weight: bfloat16 [1536, 512], P(None, 'seq'), may hold values from -0.15625 to 0.15625
- track_head_bias: bfloat16 [1, 512], P(None, 'seq'), may hold values from -4 to 4
- counts: int32 [4, 2048, 512], P('grp', 'seq'), parts along dimension 0, may hold values from 0 to 32
Outputs:
- input_grad: bfloat16 [4, 2048, 1536], P('grp', 'seq'), parts along dimension 0
- loss_value: float32 [2], P('grp'), parts along dimension 0
There are 2 independent parts, one for each index of `grp`. A program takes and returns all parts, laid end to end along the dimension named above; an argument that names none is the same for every part. Nothing has to cross between parts.
All inputs are finite; a program needn't handle non-finite values.
Results may differ from a plain program's by a relative error of at most 0.011.
Values may be sent and summed in bfloat16 or wider, within the bound.
A program may use at most 128 MiB of HBM per device.

v0:
```python
import jax
import jax.numpy as jnp
from jax import lax
from jax.sharding import PartitionSpec as P

SPAN = 8


def shifted(value, axis, steps):
    count = lax.axis_size(axis)
    initial, last = (max(0, -steps), min(count, count - steps))
    return lax.ppermute(value, axis, [(source, source + steps) for source in range(initial, last)])


def norm_rows(value_entries, gain):
    scale_inv = lax.rsqrt(jnp.mean(value_entries * value_entries, axis=-1, keepdims=True) + 1e-06)
    return value_entries * scale_inv * gain


def head_block(stream, head_full, bias_full, observed):
    logits = jnp.dot(stream, head_full, preferred_element_type=jnp.float32) + bias_full.astype(
        jnp.float32
    )
    poisson_rate = jax.nn.softplus(logits) + 0.05
    observed_f = observed.astype(jnp.float32)
    loss_total = jnp.sum(poisson_rate - observed_f * jnp.log(poisson_rate))
    logit_grad = ((1.0 - observed_f / poisson_rate) * jax.nn.sigmoid(logits)).astype(jnp.bfloat16)
    residual_gradient = lax.dot_general(
        logit_grad, head_full, (((1,), (1,)), ((), ())), preferred_element_type=jnp.float32
    )
    return (loss_total, residual_gradient)


def back_dot(left, right):
    return lax.dot_general(
        left, right, (((1,), (1,)), ((), ())), preferred_element_type=jnp.float32
    )


def shards(inputs, gain, conv_weight, proj_weight, head_weight, track_head_bias, counts):
    seq_count, row_count, window_width = inputs.shape
    flat_rows = seq_count * row_count
    track_count = counts.shape[2]
    conv_full, proj_full = (
        lax.all_gather(conv_weight, "seq", axis=1, tiled=True),
        lax.all_gather(proj_weight, "seq", axis=1, tiled=True),
    )
    inner = conv_full.shape[2]
    inputs_f = inputs.astype(jnp.float32)
    normed = norm_rows(inputs_f, gain).astype(jnp.bfloat16)
    normed_flat = normed.reshape(flat_rows, window_width)
    behind_rows = shifted(normed, "seq", SPAN).reshape(flat_rows, window_width)
    ahead_rows = shifted(normed, "seq", -SPAN).reshape(flat_rows, window_width)
    conv_pre = jnp.dot(normed_flat, conv_full[1], preferred_element_type=jnp.float32)
    conv_pre = conv_pre + jnp.dot(behind_rows, conv_full[0], preferred_element_type=jnp.float32)
    conv_pre = conv_pre + jnp.dot(ahead_rows, conv_full[2], preferred_element_type=jnp.float32)
    conv_act = jax.nn.gelu(conv_pre).astype(jnp.bfloat16)
    stream = (
        inputs_f.reshape(flat_rows, window_width)
        + jnp.dot(conv_act, proj_full, preferred_element_type=jnp.float32)
    ).astype(jnp.bfloat16)
    counts_flat = counts.reshape(flat_rows, track_count)
    head_full, bias_full = (
        lax.all_gather(head_weight, "seq", axis=1, tiled=True),
        lax.all_gather(track_head_bias, "seq", axis=1, tiled=True),
    )
    loss_total, residual_gradient = head_block(stream, head_full, bias_full, counts_flat)
    summed_loss = lax.psum(loss_total, "seq")
    loss_value = (summed_loss / (flat_rows * lax.axis_size("seq") * track_count)).reshape(1)
    act_grad = back_dot(residual_gradient.astype(jnp.bfloat16), proj_full)
    _, gelu_back = jax.vjp(jax.nn.gelu, conv_pre)
    pre_grad = gelu_back(act_grad)[0].astype(jnp.bfloat16)
    pre_three = pre_grad.reshape(seq_count, row_count, inner)
    grad_ahead = shifted(pre_three, "seq", -SPAN).reshape(flat_rows, inner)
    grad_behind = shifted(pre_three, "seq", SPAN).reshape(flat_rows, inner)
    normed_grad = back_dot(pre_grad, conv_full[1])
    normed_grad = normed_grad + back_dot(grad_ahead, conv_full[0])
    normed_grad = normed_grad + back_dot(grad_behind, conv_full[2])
    _, norm_back = jax.vjp(lambda value_entries: norm_rows(value_entries, gain), inputs_f)
    input_grad = (
        residual_gradient.reshape(seq_count, row_count, window_width)
        + norm_back(normed_grad.reshape(seq_count, row_count, window_width))[0]
    ).astype(jnp.bfloat16)
    return (input_grad, loss_value)


def solution(mesh):
    placed = (
        P("grp", "seq", None),
        P(),
        P(None, "seq", None),
        P(None, "seq"),
        P(None, "seq"),
        P(None, "seq"),
        P("grp", "seq", None),
    )
    return jax.shard_map(
        shards,
        mesh=mesh,
        in_specs=placed,
        out_specs=(P("grp", "seq", None), P("grp")),
        check_vma=False,
    )
```

profile of v0, /device:TPU:0, one launch (start us, length us, event | category | flops | bytes accessed | tf_op | source)
XLA Modules:
  0.0 252.3 jit_solution(4451681180811085461)
XLA Ops:
  7.2 0.0 copy-start.5
  7.2 0.0 all-gather.4.cloned.1.call-start
  7.2 0.7 all-gather.4.cloned.1.call-update
  7.9 0.0 all-gather.8.cloned.1.call-start
  8.0 0.7 all-gather.8.cloned.1.call-update
  8.7 0.0 all-gather.6.cloned.1.call-start
  8.7 0.7 all-gather.6.cloned.1.call-update
  9.4 1.4 multiply_reduce_fusion.1
  10.8 0.9 multiply_convert_fusion
  11.7 6.0 %collective-permute-start = (bf16[2,128,1536]{2,1,0:T(8,128)(2,1)S(1)}, bf16[2,128,1536]{2,1,0:T(8,128)(2,1)S(1)}, u32[]{:S(2)}, u32[]{:S(2)}) collective-permute-start(bf16[2,128,1536]{2,1,0:T(8,128)(2,1)S(1)} %multiply_convert_fusion), channel_id=1, source_target_pairs={{0,8},{1,9},{2,10},{3,11},{4,12},{5,13},{6,14},{7,15},{16,24},{17,... | collective-permute-start | bytes 2359304 | tf_op jit(solution)/shard_map/ppermute | solution.py:12
  17.8 1.3 collective-permute-start.1
  19.1 0.6 dynamic-slice
  20.4 0.2 dynamic-update-slice
  20.6 50.1 %all-reduce = bf16[512]{0:T(512)(128)(2,1)S(1)} all-reduce(bf16[512]{0:T(512)(128)(2,1)S(1)} %dynamic-update-slice), channel_id=1, replica_groups=mesh['grp'=2,'seq'=16] {'seq'}, use_global_device_ids=true, to_apply=%add | all-reduce | flops 512 | bytes 2048
  70.7 31.3 %all-gather.4.cloned.1.call-done = bf16[3,1536,768]{2,1,0:T(8,128)(2,1)} async-done(((bf16[3,96,768]{2,1,0:T(8,128)(2,1)}), bf16[3,1536,768]{2,1,0:T(8,128)(2,1)}) %all-gather.4.cloned.1.call-update) | async-done | bytes 7077904 | tf_op jit(solution)/shard_map/all_gather | solution.py:45
  101.9 2.4 fusion.2
  104.4 2.4 fusion.8
  106.8 2.5 fusion.7
  109.4 33.0 %all-gather.8.cloned.1.call-done = bf16[1536,512]{0,1:T(8,128)(2,1)} async-done(((bf16[1536,32]{0,1:T(8,128)(2,1)}), bf16[1536,512]{0,1:T(8,128)(2,1)}) %all-gather.8.cloned.1.call-update) | async-done | bytes 1572880 | tf_op jit(solution)/shard_map/all_gather | solution.py:64
  142.3 43.3 %all-gather.6.cloned.1.call-done = bf16[768,1536]{0,1:T(8,128)(2,1)} async-done(((bf16[768,96]{0,1:T(8,128)(2,1)}), bf16[768,1536]{0,1:T(8,128)(2,1)}) %all-gather.6.cloned.1.call-update) | async-done | bytes 2359312 | tf_op jit(solution)/shard_map/all_gather | solution.py:46
  185.7 4.6 %fusion.25 = (f32[]{:T(128)}, bf16[256,512]{1,0:T(8,128)(2,1)S(1)}) fusion(s32[2,128,512]{2,1,0:T(8,128)S(1)} %copy-done.3, f32[512]{0:T(512)S(1)} %add.86, bf16[1536,512]{0,1:T(8,128)(2,1)} %all-gather.8.cloned.1.call-done, bf16[768,1536]{0,1:T(8,128)(2,1)} %all-gather.6.cloned.1.call-done, f32[256,768]{1,0:T(8,128)S(1)} %fusion.7, ...), kind=kOutput, calls=%fused_computation.40 | convolution fusion | flops 1012072448 | bytes 6293508 | tf_op jit(solution)/shard_map/dot_general | solution.py:21
  190.2 2.1 fusion.44
  192.4 0.2 copy-done.7
  192.6 1.1 fusion.15
  193.6 1.3 collective-permute-start.2
  194.9 5.5 %collective-permute-start.3 = (bf16[2,128,768]{2,1,0:T(8,128)(2,1)S(1)}, bf16[2,128,768]{2,1,0:T(8,128)(2,1)S(1)}, u32[]{:S(2)}, u32[]{:S(2)}) collective-permute-start(bf16[2,128,768]{2,1,0:T(8,128)(2,1)S(1)} %bitcast.63), channel_id=1, source_target_pairs={{0,8},{1,9},{2,10},{3,11},{4,12},{5,13},{6,14},{7,15},{16,24},{17,... | collective-permute-start | bytes 1179656 | tf_op jit(solution)/shard_map/ppermute | solution.py:12
  200.4 3.7 %fusion.1 = f32[256,1536]{1,0:T(8,128)} fusion(bf16[256,768]{1,0:T(8,128)(2,1)S(1)} %fusion.15, bf16[3,1536,768]{2,1,0:T(8,128)(2,1)} %all-gather.4.cloned.1.call-done), kind=kOutput, calls=%fused_computation.8 | convolution fusion | flops 603979776 | bytes 4325376 | tf_op jit(solution)/shard_map/dot_general | solution.py:35
  204.1 32.7 %psum.7 = f32[]{:T(128)} all-reduce(f32[]{:T(128)} %get-tuple-element.2), channel_id=1, replica_groups=mesh['grp'=2,'seq'=16] {'seq'}, use_global_device_ids=true, to_apply=%region_3.4 | all-reduce | flops 1 | bytes 8 | tf_op jit(solution)/shard_map/psum | solution.py:68
  237.5 2.9 %convolution_add_fusion.1 = f32[256,1536]{1,0:T(8,128)S(1)} fusion(f32[256,1536]{1,0:T(8,128)} %fusion.1, bf16[256,768]{1,0:T(8,128)(2,1)S(1)} %bitcast.59, bf16[3,1536,768]{2,1,0:T(8,128)(2,1)} %all-gather.4.cloned.1.call-done), kind=kOutput, calls=%fused_computation.1 | convolution fusion | flops 604372992 | bytes 5898240 | tf_op jit(solution)/shard_map/dot_general | solution.py:35
  240.4 2.5 convolution_add_fusion
  243.0 0.3 multiply_reduce_fusion
  243.3 1.3 fusion.6
  (22 shorter events, 0.1 us)
Async XLA Ops:
  7.2 11.9 %copy-start.5 = (u32[32]{0:T(128)S(1)}, u32[32]{0:T(128)}, u32[]{:S(2)}) copy-start(u32[32]{0:T(128)} %constant.32) | copy-start | bytes 388
  7.2 3.6 %copy-start = (bf16[2,128,1536]{2,1,0:T(8,128)(2,1)S(1)}, bf16[2,128,1536]{2,1,0:T(8,128)(2,1)}, u32[]{:S(2)}) copy-start(bf16[2,128,1536]{2,1,0:T(8,128)(2,1)} %param.7) | copy-start | bytes 2359300
  7.2 13.2 %copy-start.4 = (bf16[1,32]{1,0:T(2,128)(2,1)S(1)}, bf16[1,32]{1,0:T(2,128)(2,1)}, u32[]{:S(2)}) copy-start(bf16[1,32]{1,0:T(2,128)(2,1)} %param.12) | copy-start | bytes 196
  7.2 94.7 %all-gather.4.cloned.1.call-start = ((), (), s32[]{:S(2)}) async-start(), calls=%async_computation | async-start | bytes 7520256 | tf_op jit(solution)/shard_map/all_gather | solution.py:45
  7.9 134.4 %all-gather.8.cloned.1.call-start = ((), (), s32[]{:S(2)}) async-start(), calls=%async_computation.2 | async-start | bytes 1671168 | tf_op jit(solution)/shard_map/all_gather | solution.py:64
  8.7 177.0 %all-gather.6.cloned.1.call-start = ((), (), s32[]{:S(2)}) async-start(), calls=%async_computation.1 | async-start | bytes 2506752 | tf_op jit(solution)/shard_map/all_gather | solution.py:46
  11.7 92.6 %collective-permute-start = (bf16[2,128,1536]{2,1,0:T(8,128)(2,1)S(1)}, bf16[2,128,1536]{2,1,0:T(8,128)(2,1)S(1)}, u32[]{:S(2)}, u32[]{:S(2)}) collective-permute-start(bf16[2,128,1536]{2,1,0:T(8,128)(2,1)S(1)} %multiply_convert_fusion), channel_id=1, source_target_pairs={{0,8},{1,9},{2,10},{3,11},{4,12},{5,13},{6,14},{7,15},{16,24},{17,... | collective-permute-start | bytes 2359304 | tf_op jit(solution)/shard_map/ppermute | solution.py:12
  17.8 89.1 %collective-permute-start.1 = (bf16[2,128,1536]{2,1,0:T(8,128)(2,1)S(1)}, bf16[2,128,1536]{2,1,0:T(8,128)(2,1)S(1)}, u32[]{:S(2)}, u32[]{:S(2)}) collective-permute-start(bf16[2,128,1536]{2,1,0:T(8,128)(2,1)S(1)} %multiply_convert_fusion), channel_id=1, source_target_pairs={{8,0},{9,1},{10,2},{11,3},{12,4},{13,5},{14,6},{15,7},{24,16},{25,... | collective-permute-start | bytes 2359304 | tf_op jit(solution)/shard_map/ppermute | solution.py:12
  106.8 78.8 %copy-start.3 = (s32[2,128,512]{2,1,0:T(8,128)S(1)}, s32[2,128,512]{2,1,0:T(8,128)}, u32[]{:S(2)}) copy-start(s32[2,128,512]{2,1,0:T(8,128)} %param.13) | copy-start | bytes 1572868
  109.4 80.9 %copy-start.6 = (f32[256,768]{1,0:T(8,128)}, f32[256,768]{1,0:T(8,128)S(1)}, u32[]{:S(2)}) copy-start(f32[256,768]{1,0:T(8,128)S(1)} %fusion.7) | copy-start | bytes 2359300
  190.2 2.1 copy-start.2
  190.2 2.3 copy-start.7
  193.6 43.8 %collective-permute-start.2 = (bf16[2,128,768]{2,1,0:T(8,128)(2,1)S(1)}, bf16[2,128,768]{2,1,0:T(8,128)(2,1)S(1)}, u32[]{:S(2)}, u32[]{:S(2)}) collective-permute-start(bf16[2,128,768]{2,1,0:T(8,128)(2,1)S(1)} %bitcast.62), channel_id=1, source_target_pairs={{8,0},{9,1},{10,2},{11,3},{12,4},{13,5},{14,6},{15,7},{24,16},{25,... | collective-permute-start | bytes 1179656 | tf_op jit(solution)/shard_map/ppermute | solution.py:12
  194.9 45.5 %collective-permute-start.3 = (bf16[2,128,768]{2,1,0:T(8,128)(2,1)S(1)}, bf16[2,128,768]{2,1,0:T(8,128)(2,1)S(1)}, u32[]{:S(2)}, u32[]{:S(2)}) collective-permute-start(bf16[2,128,768]{2,1,0:T(8,128)(2,1)S(1)} %bitcast.63), channel_id=1, source_target_pairs={{0,8},{1,9},{2,10},{3,11},{4,12},{5,13},{6,14},{7,15},{16,24},{17,... | collective-permute-start | bytes 1179656 | tf_op jit(solution)/shard_map/ppermute | solution.py:12
  240.4 2.5 %copy-start.1 = (f32[1536]{0:T(1024)S(1)}, f32[1536]{0:T(1024)}, u32[]{:S(2)}) copy-start(f32[1536]{0:T(1024)} %param.8) | copy-start | bytes 18436
Sparse Core Ops, SparseCore 0:
  10.3 91.5 all-gather.3
  104.2 38.0 all-gather.7
  144.6 41.0 all-gather.5
where the time goes:
time: 253 us; the launch traced here: 252 us
  waiting for transfers between devices  110 us (43%)
  blocking collectives  82.7 us (33%)
  matrix products  24.3 us (10%)
  between operations  16.4 us (6%)
  starting transfers between devices  14.2 us (6%)
  other arithmetic  4.01 us (2%)
    unnamed x1, blocking collectives  50.1 us
    all_gather x1, waiting for transfers between devices, shards(): lax.all_gather(proj_weight, 'seq', axis=1, tiled=True)  43.3 us
    all_gather x1, waiting for transfers between devices, shards(): lax.all_gather(head_weight, 'seq', axis=1, tiled=True)  33 us
    psum x1, blocking collectives, shards(): summed_loss = lax.psum(loss_total, 'seq')  32.7 us
    all_gather x1, waiting for transfers between devices, shards(): lax.all_gather(conv_weight, 'seq', axis=1, tiled=True)  31.3 us
    ppermute x4, starting transfers between devices, shifted(): lax.ppermute(value, axis, [(source, source + steps) for source in range(i...  14.1 us
    dot_general x4, matrix products, back_dot(): lax.dot_general(left, right, (((1,), (1,)), ((), ())), preferred_element_...  10.2 us
  transfers between devices with their start and end apart: 7, of which 3 were waited for; matrix products, arithmetic and copies ran while one was open for 7% of the time, Pallas kernels for 0%

commit v1 on v0

--- a/solution.py
+++ b/solution.py
@@ -43,7 +43,12 @@
     track_count = counts.shape[2]
     conv_full, proj_full = (
         lax.all_gather(conv_weight, "seq", axis=1, tiled=True),
-        lax.all_gather(proj_weight, "seq", axis=1, tiled=True),
+        jnp.concatenate(
+            lax.all_to_all(
+                jnp.stack([proj_weight for _ in range(lax.axis_size("seq"))], 0), "seq", 0, 0
+            ),
+            1,
+        ),
     )
     inner = conv_full.shape[2]
     inputs_f = inputs.astype(jnp.float32)

time: 253 us -> 245 us (0.968)
  waiting for transfers between devices: 110 us -> 41.5 us
  blocking collectives: 82.7 us -> 132 us
  starting transfers between devices: 14.2 us -> 21.3 us
  local copies, waits for them, and re-layouts: 1.05 us -> 3.63 us
    unnamed x1, blocking collectives: 50.1 us -> 99.7 us
    all_gather x1 -> x0, waiting for transfers between devices: 43.3 us -> none  [shards(): lax.all_gather(proj_weight, 'seq', axis=1, tiled=True)]
    all_gather x1, waiting for transfers between devices: 31.3 us -> 8.27 us  [shards(): lax.all_gather(conv_weight, 'seq', axis=1, tiled=True)]
    all_gather x1, waiting for transfers between devices: 33 us -> 24.6 us  [shards(): lax.all_gather(head_weight, 'seq', axis=1, tiled=True)]
    all_to_all x0 -> x1, starting transfers between devices: none -> 7.52 us  [shards(): lax.all_to_all(jnp.stack([proj_weight for _ in range(lax.axis_size('seq')...]
    ppermute x4, waiting for transfers between devices: 0.01 us -> 7.17 us  [shifted(): lax.ppermute(value, axis, [(source, source + steps) for source in range(i...]
    another operation x0 -> x1, local copies, waits for them, and re-layouts: none -> 2.6 us  [shards(): jnp.stack([proj_weight for _ in range(lax.axis_size('seq'))], 0)]
  transfers between devices with their start and end apart: 7 -> 7, of which waited for: 3 -> 3; matrix products, arithmetic and copies ran while one was open for 7% -> 8% of each run, Pallas kernels for 0% -> 0%
where the time goes in v1:
time: 245 us
  blocking collectives  132 us (54%)
  waiting for transfers between devices  41.5 us (17%)
  matrix products  26.3 us (11%)
  starting transfers between devices  21.3 us (9%)
  between operations  16.6 us (7%)
  local copies, waits for them, and re-layouts  3.63 us (1%)
  other arithmetic  3.05 us (1%)
    unnamed x1, blocking collectives  99.7 us
    psum x1, blocking collectives, shards(): summed_loss = lax.psum(loss_total, 'seq')  32.7 us
    all_gather x1, waiting for transfers between devices, shards(): lax.all_gather(head_weight, 'seq', axis=1, tiled=True)  24.6 us
    ppermute x4, starting transfers between devices, shifted(): lax.ppermute(value, axis, [(source, source + steps) for source in range(i...  13.7 us
    dot_general x4, matrix products, back_dot(): lax.dot_general(left, right, (((1,), (1,)), ((), ())), preferred_element_...  10.2 us
    all_gather x1, waiting for transfers between devices, shards(): lax.all_gather(conv_weight, 'seq', axis=1, tiled=True)  8.27 us
    all_to_all x1, starting transfers between devices, shards(): lax.all_to_all(jnp.stack([proj_weight for _ in range(lax.axis_size('seq')...  7.52 us
    ppermute x4, waiting for transfers between devices, shifted(): lax.ppermute(value, axis, [(source, source + steps) for source in range(i...  7.17 us
  transfers between devices with their start and end apart: 7, of which 3 were waited for; matrix products, arithmetic and copies ran while one was open for 8% of the time, Pallas kernels for 0%

profile of v1, /device:TPU:0, one launch (start us, length us, event | category | flops | bytes accessed | tf_op | source)
XLA Modules:
  0.0 244.8 jit_solution(18380090636796836960)
XLA Ops:
  7.2 0.0 all-gather.3.cloned.1.call-start
  7.2 0.7 all-gather.3.cloned.1.call-update
  7.9 2.6 %stack.2 = bf16[16,768,96]{1,2,0:T(8,128)(2,1)} broadcast(bf16[768,96]{0,1:T(8,128)(2,1)} %param.10), dimensions={1,2} | broadcast | bytes 2506752 | tf_op jit(solution)/shard_map/stack | solution.py:48
  10.5 7.5 %all-to-all-start = ((bf16[16,768,96]{1,2,0:T(8,128)(2,1)}), bf16[16,768,96]{1,2,0:T(8,128)(2,1)S(1)}, u32[]{:S(2)}, u32[]{:S(2)}) async-start(bf16[16,768,96]{1,2,0:T(8,128)(2,1)} %stack.2), calls=%async_computation | async-start | bytes 4718592 | tf_op jit(solution)/shard_map/all_to_all | solution.py:47
  18.0 0.0 copy-start.5
  18.0 0.0 all-gather.5.cloned.1.call-start
  18.1 0.7 all-gather.5.cloned.1.call-update
  18.8 0.2 multiply_reduce_fusion.1
  19.1 1.1 multiply_convert_fusion
  20.2 5.6 %collective-permute-start = (bf16[2,128,1536]{2,1,0:T(8,128)(2,1)}, bf16[2,128,1536]{2,1,0:T(8,128)(2,1)}, u32[]{:S(2)}, u32[]{:S(2)}) collective-permute-start(bf16[2,128,1536]{2,1,0:T(8,128)(2,1)} %multiply_convert_fusion), channel_id=1, source_target_pairs={{0,8},{1,9},{2,10},{3,11},{4,12},{5,13},{6,14},{7,15},{16,24},{17,... | collective-permute-start | bytes 2359304 | tf_op jit(solution)/shard_map/ppermute | solution.py:12
  25.8 1.3 collective-permute-start.1
  27.1 0.6 dynamic-slice
  28.4 0.2 dynamic-update-slice
  28.6 99.7 %all-reduce = bf16[512]{0:T(512)(128)(2,1)S(1)} all-reduce(bf16[512]{0:T(512)(128)(2,1)S(1)} %dynamic-update-slice), channel_id=1, replica_groups=mesh['grp'=2,'seq'=16] {'seq'}, use_global_device_ids=true, to_apply=%add | all-reduce | flops 512 | bytes 2048
  128.3 8.3 %all-gather.3.cloned.1.call-done = bf16[3,1536,768]{2,1,0:T(8,128)(2,1)} async-done(((bf16[3,96,768]{2,1,0:T(8,128)(2,1)}), bf16[3,1536,768]{2,1,0:T(8,128)(2,1)}) %all-gather.3.cloned.1.call-update) | async-done | bytes 7077904 | tf_op jit(solution)/shard_map/all_gather | solution.py:45
  136.6 2.7 %fusion.2 = f32[256,768]{1,0:T(8,128)S(1)} fusion(bf16[256,1536]{1,0:T(8,128)(2,1)} %bitcast.2, bf16[3,1536,768]{2,1,0:T(8,128)(2,1)} %all-gather.3.cloned.1.call-done), kind=kOutput, calls=%fused_computation.9 | convolution fusion | flops 603979776 | bytes 3932160 | tf_op jit(solution)/shard_map/dot_general | solution.py:59
  139.3 2.7 %fusion.8 = f32[256,768]{1,0:T(8,128)S(1)} fusion(f32[256,768]{1,0:T(8,128)S(1)} %fusion.2, bf16[256,1536]{1,0:T(8,128)(2,1)} %bitcast.4, bf16[3,1536,768]{2,1,0:T(8,128)(2,1)} %all-gather.3.cloned.1.call-done), kind=kOutput, calls=%fused_computation.19 | convolution fusion | flops 604176384 | bytes 4718592 | tf_op jit(solution)/shard_map/dot_general | solution.py:60
  142.0 7.2 %collective-permute-done.1 = bf16[2,128,1536]{2,1,0:T(8,128)(2,1)} collective-permute-done((bf16[2,128,1536]{2,1,0:T(8,128)(2,1)}, bf16[2,128,1536]{2,1,0:T(8,128)(2,1)}, u32[]{:S(2)}, u32[]{:S(2)}) %collective-permute-start.1) | collective-permute-done | bytes 786464 | tf_op jit(solution)/shard_map/ppermute | solution.py:12
  149.2 3.6 %fusion.7 = f32[256,768]{1,0:T(8,128)} fusion(f32[256,768]{1,0:T(8,128)S(1)} %fusion.8, bf16[256,1536]{1,0:T(8,128)(2,1)} %bitcast.6, bf16[3,1536,768]{2,1,0:T(8,128)(2,1)} %all-gather.3.cloned.1.call-done), kind=kOutput, calls=%fused_computation.18 | convolution fusion | flops 604176384 | bytes 4718592 | tf_op jit(solution)/shard_map/dot_general | solution.py:61
  152.8 24.6 %all-gather.5.cloned.1.call-done = bf16[1536,512]{0,1:T(8,128)(2,1)} async-done(((bf16[1536,32]{0,1:T(8,128)(2,1)}), bf16[1536,512]{0,1:T(8,128)(2,1)}) %all-gather.5.cloned.1.call-update) | async-done | bytes 1572880 | tf_op jit(solution)/shard_map/all_gather | solution.py:69
  177.4 5.0 %fusion.25 = (f32[]{:T(128)}, bf16[256,512]{1,0:T(8,128)(2,1)S(1)}) fusion(s32[2,128,512]{2,1,0:T(8,128)} %param.13, f32[512]{0:T(512)S(1)} %add.86, bf16[1536,512]{0,1:T(8,128)(2,1)} %all-gather.5.cloned.1.call-done, bf16[768,1536]{0,1:T(8,128)(2,1)S(1)} %bitcast.60, f32[256,768]{1,0:T(8,128)} %fusion.7, bf16[256,1536]{1,0:T(8,128)(2,1)S(1)} %bitcast.58), kind=kOutput, calls=%fused_computation.40 | convolution fusion | flops 1012072448 | bytes 6293508 | tf_op jit(solution)/shard_map/dot_general | solution.py:21
  182.4 2.1 fusion.44
  184.6 0.2 copy-done.6
  184.8 1.1 fusion.15
  185.8 1.3 collective-permute-start.2
  187.1 5.5 %collective-permute-start.3 = (bf16[2,128,768]{2,1,0:T(8,128)(2,1)S(1)}, bf16[2,128,768]{2,1,0:T(8,128)(2,1)S(1)}, u32[]{:S(2)}, u32[]{:S(2)}) collective-permute-start(bf16[2,128,768]{2,1,0:T(8,128)(2,1)S(1)} %bitcast.65), channel_id=1, source_target_pairs={{0,8},{1,9},{2,10},{3,11},{4,12},{5,13},{6,14},{7,15},{16,24},{17,... | collective-permute-start | bytes 1179656 | tf_op jit(solution)/shard_map/ppermute | solution.py:12
  192.6 3.7 %fusion.1 = f32[256,1536]{1,0:T(8,128)} fusion(bf16[256,768]{1,0:T(8,128)(2,1)S(1)} %fusion.15, bf16[3,1536,768]{2,1,0:T(8,128)(2,1)} %all-gather.3.cloned.1.call-done), kind=kOutput, calls=%fused_computation.8 | convolution fusion | flops 603979776 | bytes 4325376 | tf_op jit(solution)/shard_map/dot_general | solution.py:35
  196.3 32.7 %psum.7 = f32[]{:T(128)} all-reduce(f32[]{:T(128)} %get-tuple-element.2), channel_id=1, replica_groups=mesh['grp'=2,'seq'=16] {'seq'}, use_global_device_ids=true, to_apply=%region_3.4 | all-reduce | flops 1 | bytes 8 | tf_op jit(solution)/shard_map/psum | solution.py:73
  229.6 2.9 %convolution_add_fusion.1 = f32[256,1536]{1,0:T(8,128)S(1)} fusion(f32[256,1536]{1,0:T(8,128)} %fusion.1, bf16[256,768]{1,0:T(8,128)(2,1)S(1)} %bitcast.63, bf16[3,1536,768]{2,1,0:T(8,128)(2,1)} %all-gather.3.cloned.1.call-done), kind=kOutput, calls=%fused_computation.1 | convolution fusion | flops 604372992 | bytes 5898240 | tf_op jit(solution)/shard_map/dot_general | solution.py:35
  232.6 2.5 %convolution_add_fusion = f32[256,1536]{1,0:T(8,128)S(1)} fusion(f32[256,1536]{1,0:T(8,128)S(1)} %convolution_add_fusion.1, bf16[256,768]{1,0:T(8,128)(2,1)S(1)} %bitcast.62, bf16[3,1536,768]{2,1,0:T(8,128)(2,1)} %all-gather.3.cloned.1.call-done), kind=kOutput, calls=%fused_computation | convolution fusion | flops 604372992 | bytes 5898240 | tf_op jit(solution)/shard_map/dot_general | solution.py:35
  235.1 0.3 multiply_reduce_fusion
  235.4 1.3 fusion.6
  (20 shorter events, 0.1 us)
Async XLA Ops:
  7.2 129.5 %all-gather.3.cloned.1.call-start = ((), (), s32[]{:S(2)}) async-start(), calls=%async_computation.1 | async-start | bytes 7520256 | tf_op jit(solution)/shard_map/all_gather | solution.py:45
  10.5 8.3 %copy-start = (bf16[2,128,1536]{2,1,0:T(8,128)(2,1)S(1)}, bf16[2,128,1536]{2,1,0:T(8,128)(2,1)}, u32[]{:S(2)}) copy-start(bf16[2,128,1536]{2,1,0:T(8,128)(2,1)} %param.7) | copy-start | bytes 2359300
  10.5 8.6 %copy-start.3 = (f32[1536]{0:T(1024)S(1)}, f32[1536]{0:T(1024)}, u32[]{:S(2)}) copy-start(f32[1536]{0:T(1024)} %param.8) | copy-start | bytes 18436
  10.5 166.9 %all-to-all-start = ((bf16[16,768,96]{1,2,0:T(8,128)(2,1)}), bf16[16,768,96]{1,2,0:T(8,128)(2,1)S(1)}, u32[]{:S(2)}, u32[]{:S(2)}) async-start(bf16[16,768,96]{1,2,0:T(8,128)(2,1)} %stack.2), calls=%async_computation | async-start | bytes 4718592 | tf_op jit(solution)/shard_map/all_to_all | solution.py:47
  18.0 9.1 %copy-start.5 = (u32[32]{0:T(128)S(1)}, u32[32]{0:T(128)}, u32[]{:S(2)}) copy-start(u32[32]{0:T(128)} %constant.32) | copy-start | bytes 388
  18.0 10.3 %copy-start.4 = (bf16[1,32]{1,0:T(2,128)(2,1)S(1)}, bf16[1,32]{1,0:T(2,128)(2,1)}, u32[]{:S(2)}) copy-start(bf16[1,32]{1,0:T(2,128)(2,1)} %param.12) | copy-start | bytes 196
  18.0 159.4 %all-gather.5.cloned.1.call-start = ((), (), s32[]{:S(2)}) async-start(), calls=%async_computation.2 | async-start | bytes 1671168 | tf_op jit(solution)/shard_map/all_gather | solution.py:69
  20.2 119.1 %collective-permute-start = (bf16[2,128,1536]{2,1,0:T(8,128)(2,1)}, bf16[2,128,1536]{2,1,0:T(8,128)(2,1)}, u32[]{:S(2)}, u32[]{:S(2)}) collective-permute-start(bf16[2,128,1536]{2,1,0:T(8,128)(2,1)} %multiply_convert_fusion), channel_id=1, source_target_pairs={{0,8},{1,9},{2,10},{3,11},{4,12},{5,13},{6,14},{7,15},{16,24},{17,... | collective-permute-start | bytes 2359304 | tf_op jit(solution)/shard_map/ppermute | solution.py:12
  25.8 123.4 %collective-permute-start.1 = (bf16[2,128,1536]{2,1,0:T(8,128)(2,1)}, bf16[2,128,1536]{2,1,0:T(8,128)(2,1)}, u32[]{:S(2)}, u32[]{:S(2)}) collective-permute-start(bf16[2,128,1536]{2,1,0:T(8,128)(2,1)} %multiply_convert_fusion), channel_id=1, source_target_pairs={{8,0},{9,1},{10,2},{11,3},{12,4},{13,5},{14,6},{15,7},{24,16},{25,... | collective-permute-start | bytes 2359304 | tf_op jit(solution)/shard_map/ppermute | solution.py:12
  177.4 5.0 %copy-start.1 = (bf16[16,768,96]{1,2,0:T(8,128)(2,1)}, bf16[16,768,96]{1,2,0:T(8,128)(2,1)S(1)}, u32[]{:S(2)}) copy-start(bf16[16,768,96]{1,2,0:T(8,128)(2,1)S(1)} %all-to-all-done) | copy-start | bytes 7077892
  182.4 2.1 copy-start.2
  182.4 2.3 copy-start.6
  185.8 43.8 %collective-permute-start.2 = (bf16[2,128,768]{2,1,0:T(8,128)(2,1)S(1)}, bf16[2,128,768]{2,1,0:T(8,128)(2,1)S(1)}, u32[]{:S(2)}, u32[]{:S(2)}) collective-permute-start(bf16[2,128,768]{2,1,0:T(8,128)(2,1)S(1)} %bitcast.64), channel_id=1, source_target_pairs={{8,0},{9,1},{10,2},{11,3},{12,4},{13,5},{14,6},{15,7},{24,16},{25,... | collective-permute-start | bytes 1179656 | tf_op jit(solution)/shard_map/ppermute | solution.py:12
  187.1 45.4 %collective-permute-start.3 = (bf16[2,128,768]{2,1,0:T(8,128)(2,1)S(1)}, bf16[2,128,768]{2,1,0:T(8,128)(2,1)S(1)}, u32[]{:S(2)}, u32[]{:S(2)}) collective-permute-start(bf16[2,128,768]{2,1,0:T(8,128)(2,1)S(1)} %bitcast.65), channel_id=1, source_target_pairs={{0,8},{1,9},{2,10},{3,11},{4,12},{5,13},{6,14},{7,15},{16,24},{17,... | collective-permute-start | bytes 1179656 | tf_op jit(solution)/shard_map/ppermute | solution.py:12
Sparse Core Ops, SparseCore 0:
  10.3 126.3 all-gather.2
  138.9 38.4 all-gather.4
